TPU v7x, 32 devices: a whole 2x2x4 slice. The times are simulated.
32 devices in a mesh: freq: 2 (over x), tile: 16 (over z, y, core).
Axes of the slice: x: 2, y: 2, z: 4, core: 2. Of those that a mesh axis runs over, the one named last changes fastest.
Arguments:
- model_start: float32 [2, 4096, 128], P('freq', 'tile'), may hold values from -6 to 6
- data: bfloat16 [2, 4096, 128], P('freq', 'tile'), may hold values from -6 to 6
- col_factors: bfloat16 [2, 128, 2, 112, 256], P('freq', 'tile'), may hold values from -0.375 to 0.375
- row_factors: bfloat16 [2, 128, 2, 112, 256], P('freq', 'tile'), may hold values from -0.1875 to 0.1875
- ranks: int32 [2, 16, 8], P('freq'), may hold values from 16 to 112
- gate_window: int32 [64, 2], replicated, may hold values from 0 to 2047, as said below
- step_sizes: float32 [2], P('freq'), may hold values from 0.2 to 0.6
Outputs:
- model_final: float32 [2, 4096, 128], P('freq', 'tile')
Inputs may be any that keep to these rules, and one draw needn't show every extreme that they name: `gate_window`: each row is (start, end) with 256 <= end - start <= 1024.
All inputs are finite; a program needn't handle non-finite values.
Results may differ from a plain program's by a relative error of at most 0.0085.
Values may be sent and summed in bfloat16 or wider, within the bound.
A program may use at most 64 MiB of HBM per device.

v0:
```python
import math

import jax
import jax.numpy as jnp
from jax import lax
from jax.sharding import PartitionSpec as P

NT = 2048
ITERS = 2


def shifted(value, axis, steps):
    count = lax.axis_size(axis)
    leading, last = (max(0, -steps), min(count, count - steps))
    return lax.ppermute(value, axis, [(source, source + steps) for source in range(leading, last)])


def rotate(z):
    half = z.shape[-1] // 2
    return jnp.concatenate([-z[..., half:], z[..., :half]], axis=-1)


def gate_matrix(window, count):
    start = window[:, 0].astype(jnp.float32)
    span = (window[:, 1] - window[:, 0]).astype(jnp.float32)
    freqs = jnp.arange(count, dtype=jnp.float32)
    delta = freqs[:, None] - freqs[None, :]
    theta = 2.0 * math.pi * delta / NT
    safe = jnp.where(delta == 0.0, 1.0, jnp.sin(theta / 2.0))
    magnitude = jnp.where(
        (delta == 0.0)[:, :, None],
        span[None, None, :] / NT,
        jnp.sin(theta[:, :, None] * span[None, None, :] / 2.0) / (NT * safe[:, :, None]),
    )
    phase = theta[:, :, None] * (start[None, None, :] + (span[None, None, :] - 1.0) / 2.0)
    return (magnitude * jnp.cos(phase), magnitude * jnp.sin(phase))


def left_dot(factor, values):
    return lax.dot_general(
        factor, values, (((0,), (0,)), ((), ())), preferred_element_type=jnp.float32
    )


def complex_mix(coeff_re, coeff_im, values):
    width = values.shape[-1] // 2
    vals_re = values[..., :width]
    vals_im = values[..., width:]
    out_re = jnp.sum(coeff_re[:, None, :] * vals_re - coeff_im[:, None, :] * vals_im, axis=0)
    out_im = jnp.sum(coeff_re[:, None, :] * vals_im + coeff_im[:, None, :] * vals_re, axis=0)
    return jnp.concatenate([out_re, out_im], axis=-1)


def forward_hop(block, amount):
    return shifted(block, "tile", amount)


def adjoint_hop(block, amount):
    return shifted(block, "tile", amount)


def deliver_hops(pieces, moves, hopper):
    result = list(pieces)
    reach = max(max((abs(amount) for amount in moves)), 1)
    for level in range(reach.bit_length()):
        for heading in (1, -1):
            chosen = [
                index
                for index, amount in enumerate(moves)
                if amount * heading > 0 and amount * heading >> level & 1
            ]
            if chosen:
                moved = hopper(
                    jnp.stack([result[index] for index in chosen]), heading * (1 << level)
                )
                for place, index in enumerate(chosen):
                    result[index] = moved[place]
    return result


def on_device(model_start, data, col_factors, row_factors, ranks, gate_window, step_sizes):
    ntile = lax.axis_size("tile")
    nfreq = lax.axis_size("freq")
    myself = lax.axis_index("tile")
    my_freq = lax.axis_index("freq")
    slots = ranks.shape[2]
    levels = col_factors.shape[3]
    tile_rows = col_factors.shape[4]
    center = slots // 2
    moves = [index - center for index in range(slots)]
    backward = [-amount for amount in moves]
    factors_v = col_factors[0]
    factors_u = row_factors[0]
    v_real = factors_v[:, 0].reshape(slots * levels, tile_rows)
    v_imag = factors_v[:, 1].reshape(slots * levels, tile_rows)
    u_real = factors_u[:, 0].reshape(slots * levels, tile_rows)
    u_imag = factors_u[:, 1].reshape(slots * levels, tile_rows)
    rank_table = ranks[0]
    devices = jnp.arange(ntile, dtype=jnp.int32)
    anchors = myself - (jnp.arange(slots, dtype=jnp.int32) - center)
    holder = devices[:, None] == anchors[None, :]
    row_ranks = jnp.sum(jnp.where(holder, rank_table, 0), axis=0)
    my_ranks = lax.dynamic_index_in_dim(rank_table, myself, 0, keepdims=False)
    level_ids = jnp.arange(levels, dtype=jnp.int32)
    col_mask = (level_ids[None, :] < my_ranks[:, None]).astype(jnp.float32)
    row_mask = (level_ids[None, :] < row_ranks[:, None]).astype(jnp.float32)
    gate_re, gate_im = gate_matrix(gate_window, nfreq)
    stepping = step_sizes[0]
    model = model_start[0]
    observed = data[0].astype(jnp.float32)
    width = model.shape[-1]
    for step in range(ITERS):
        model_bf = model.astype(jnp.bfloat16)
        coef = jnp.dot(v_real, model_bf, preferred_element_type=jnp.float32) + jnp.dot(
            v_imag, rotate(model_bf), preferred_element_type=jnp.float32
        )
        coef = (coef.reshape(slots, levels, width) * col_mask[:, :, None]).astype(jnp.bfloat16)
        outgoing = [coef[index] for index in range(slots)]
        arrived = deliver_hops(outgoing, moves, forward_hop)
        placed = jnp.stack(arrived).reshape(slots * levels, width)
        image = left_dot(u_real, placed) + left_dot(u_imag, rotate(placed))
        resid = (image - observed).astype(jnp.bfloat16)
        return_trip = jnp.dot(u_real, resid, preferred_element_type=jnp.float32) - jnp.dot(
            u_imag, rotate(resid), preferred_element_type=jnp.float32
        )
        return_trip = (return_trip.reshape(slots, levels, width) * row_mask[:, :, None]).astype(
            jnp.bfloat16
        )
        sending = [return_trip[index] for index in range(slots)]
        landed = deliver_hops(sending, backward, adjoint_hop)
        gathered = jnp.stack(landed).reshape(slots * levels, width)
        grad = left_dot(v_real, gathered) - left_dot(v_imag, rotate(gathered))
        updated = model - stepping * grad
        row_re = lax.dynamic_index_in_dim(gate_re, my_freq, 0, keepdims=False)
        row_im = lax.dynamic_index_in_dim(gate_im, my_freq, 0, keepdims=False)
        model = complex_mix(
            row_re, row_im, lax.all_gather(updated[None], "freq", axis=0, tiled=True)
        )
    return model[None]


def solution(mesh):
    return jax.shard_map(
        on_device,
        mesh=mesh,
        in_specs=(
            P("freq", "tile", None),
            P("freq", "tile", None),
            P("freq", "tile", None, None, None),
            P("freq", "tile", None, None, None),
            P("freq", None, None),
            P(),
            P("freq"),
        ),
        out_specs=P("freq", "tile", None),
        check_vma=False,
    )
```

profile of v0, /device:TPU:23, one launch (start us, length us, event | category | flops | bytes accessed | tf_op | source)
XLA Modules:
  0.0 123.5 jit_solution(9287751117837560850)
XLA Ops:
  4.0 2.1 %collective-permute-start = (bf16[1,112,128]{2,1,0:T(8,128)(2,1)S(1)}, bf16[1,112,128]{2,1,0:T(8,128)(2,1)S(1)}, u32[]{:S(2)}, u32[]{:S(2)}) collective-permute-start(bf16[1,112,128]{2,1,0:T(8,128)(2,1)S(1)} %get-tuple-element.54), channel_id=1, source_target_pairs={{4,0},{5,1},{6,2},{7,3},{8,4},{9,5},{10,6},{11,7},{12,8},{13,9},{1... | collective-permute-start | bytes 86024 | tf_op jit(solution)/shard_map/ppermute | solution.py:15
  6.2 2.9 %collective-permute-start.1 = (bf16[2,112,128]{2,1,0:T(8,128)(2,1)S(1)}, bf16[2,112,128]{2,1,0:T(8,128)(2,1)S(1)}, u32[]{:S(2)}, u32[]{:S(2)}) collective-permute-start(bf16[2,112,128]{2,1,0:T(8,128)(2,1)S(1)} %pad_maximum_fusion.1), channel_id=1, source_target_pairs={{1,0},{2,1},{3,2},{4,3},{5,4},{6,5},{7,6},{8,7},{9,8},{10,9},{11,1... | collective-permute-start | bytes 172040 | tf_op jit(solution)/shard_map/ppermute | solution.py:15
  10.0 2.6 %collective-permute-done.1 = bf16[2,112,128]{2,1,0:T(8,128)(2,1)S(1)} collective-permute-done((bf16[2,112,128]{2,1,0:T(8,128)(2,1)S(1)}, bf16[2,112,128]{2,1,0:T(8,128)(2,1)S(1)}, u32[]{:S(2)}, u32[]{:S(2)}) %collective-permute-start.1) | collective-permute-done | bytes 57376 | tf_op jit(solution)/shard_map/ppermute | solution.py:15
  12.6 1.9 %collective-permute-start.2 = (bf16[2,112,128]{2,1,0:T(8,128)(2,1)S(1)}, bf16[2,112,128]{2,1,0:T(8,128)(2,1)S(1)}, u32[]{:S(2)}, u32[]{:S(2)}) collective-permute-start(bf16[2,112,128]{2,1,0:T(8,128)(2,1)S(1)} %pad_maximum_fusion.2), channel_id=1, source_target_pairs={{2,0},{3,1},{4,2},{5,3},{6,4},{7,5},{8,6},{9,7},{10,8},{11,9},{12,... | collective-permute-start | bytes 172040 | tf_op jit(solution)/shard_map/ppermute | solution.py:15
  14.5 3.9 %collective-permute-done.2 = bf16[2,112,128]{2,1,0:T(8,128)(2,1)S(1)} collective-permute-done((bf16[2,112,128]{2,1,0:T(8,128)(2,1)S(1)}, bf16[2,112,128]{2,1,0:T(8,128)(2,1)S(1)}, u32[]{:S(2)}, u32[]{:S(2)}) %collective-permute-start.2) | collective-permute-done | bytes 57376 | tf_op jit(solution)/shard_map/ppermute | solution.py:15
  18.5 2.6 %collective-permute-start.3 = (bf16[2,112,128]{2,1,0:T(8,128)(2,1)S(1)}, bf16[2,112,128]{2,1,0:T(8,128)(2,1)S(1)}, u32[]{:S(2)}, u32[]{:S(2)}) collective-permute-start(bf16[2,112,128]{2,1,0:T(8,128)(2,1)S(1)} %pad_maximum_fusion.3), channel_id=1, source_target_pairs={{0,1},{1,2},{2,3},{3,4},{4,5},{5,6},{6,7},{7,8},{8,9},{9,10},{10,1... | collective-permute-start | bytes 172040 | tf_op jit(solution)/shard_map/ppermute | solution.py:15
  22.3 1.9 %collective-permute-start.4 = (bf16[2,112,128]{2,1,0:T(8,128)(2,1)S(1)}, bf16[2,112,128]{2,1,0:T(8,128)(2,1)S(1)}, u32[]{:S(2)}, u32[]{:S(2)}) collective-permute-start(bf16[2,112,128]{2,1,0:T(8,128)(2,1)S(1)} %pad_maximum_fusion.4), channel_id=1, source_target_pairs={{0,2},{1,3},{2,4},{3,5},{4,6},{5,7},{6,8},{7,9},{8,10},{9,11},{10,... | collective-permute-start | bytes 172040 | tf_op jit(solution)/shard_map/ppermute | solution.py:15
  24.3 2.9 %collective-permute-done.4 = bf16[2,112,128]{2,1,0:T(8,128)(2,1)S(1)} collective-permute-done((bf16[2,112,128]{2,1,0:T(8,128)(2,1)S(1)}, bf16[2,112,128]{2,1,0:T(8,128)(2,1)S(1)}, u32[]{:S(2)}, u32[]{:S(2)}) %collective-permute-start.4) | collective-permute-done | bytes 57376 | tf_op jit(solution)/shard_map/ppermute | solution.py:15
  29.1 7.2 %collective-permute-start.6 = (bf16[2,112,128]{2,1,0:T(8,128)(2,1)S(1)}, bf16[2,112,128]{2,1,0:T(8,128)(2,1)S(1)}, u32[]{:S(2)}, u32[]{:S(2)}) collective-permute-start(bf16[2,112,128]{2,1,0:T(8,128)(2,1)S(1)} %pad_maximum_fusion.5), channel_id=1, source_target_pairs={{0,1},{1,2},{2,3},{3,4},{4,5},{5,6},{6,7},{7,8},{8,9},{9,10},{10,1... | collective-permute-start | bytes 172040 | tf_op jit(solution)/shard_map/ppermute | solution.py:15
  36.3 1.9 %collective-permute-start.5 = (bf16[1,112,128]{2,1,0:T(8,128)(2,1)S(1)}, bf16[1,112,128]{2,1,0:T(8,128)(2,1)S(1)}, u32[]{:S(2)}, u32[]{:S(2)}) collective-permute-start(bf16[1,112,128]{2,1,0:T(8,128)(2,1)S(1)} %get-tuple-element.44), channel_id=1, source_target_pairs={{0,4},{1,5},{2,6},{3,7},{4,8},{5,9},{6,10},{7,11},{8,12},{9,13},{1... | collective-permute-start | bytes 86024 | tf_op jit(solution)/shard_map/ppermute | solution.py:15
  38.3 1.9 %collective-permute-start.7 = (bf16[2,112,128]{2,1,0:T(8,128)(2,1)S(1)}, bf16[2,112,128]{2,1,0:T(8,128)(2,1)S(1)}, u32[]{:S(2)}, u32[]{:S(2)}) collective-permute-start(bf16[2,112,128]{2,1,0:T(8,128)(2,1)S(1)} %pad_maximum_fusion.6), channel_id=1, source_target_pairs={{0,2},{1,3},{2,4},{3,5},{4,6},{5,7},{6,8},{7,9},{8,10},{9,11},{10,... | collective-permute-start | bytes 172040 | tf_op jit(solution)/shard_map/ppermute | solution.py:15
  41.0 3.2 %collective-permute-done.7 = bf16[2,112,128]{2,1,0:T(8,128)(2,1)S(1)} collective-permute-done((bf16[2,112,128]{2,1,0:T(8,128)(2,1)S(1)}, bf16[2,112,128]{2,1,0:T(8,128)(2,1)S(1)}, u32[]{:S(2)}, u32[]{:S(2)}) %collective-permute-start.7) | collective-permute-done | bytes 57376 | tf_op jit(solution)/shard_map/ppermute | solution.py:15
  44.2 3.0 %collective-permute-start.8 = (bf16[2,112,128]{2,1,0:T(8,128)(2,1)S(1)}, bf16[2,112,128]{2,1,0:T(8,128)(2,1)S(1)}, u32[]{:S(2)}, u32[]{:S(2)}) collective-permute-start(bf16[2,112,128]{2,1,0:T(8,128)(2,1)S(1)} %pad_maximum_fusion.7), channel_id=1, source_target_pairs={{1,0},{2,1},{3,2},{4,3},{5,4},{6,5},{7,6},{8,7},{9,8},{10,9},{11,1... | collective-permute-start | bytes 172040 | tf_op jit(solution)/shard_map/ppermute | solution.py:15
  48.0 3.9 %collective-permute-done.8 = bf16[2,112,128]{2,1,0:T(8,128)(2,1)S(1)} collective-permute-done((bf16[2,112,128]{2,1,0:T(8,128)(2,1)S(1)}, bf16[2,112,128]{2,1,0:T(8,128)(2,1)S(1)}, u32[]{:S(2)}, u32[]{:S(2)}) %collective-permute-start.8) | collective-permute-done | bytes 57376 | tf_op jit(solution)/shard_map/ppermute | solution.py:15
  51.9 1.9 %collective-permute-start.9 = (bf16[2,112,128]{2,1,0:T(8,128)(2,1)S(1)}, bf16[2,112,128]{2,1,0:T(8,128)(2,1)S(1)}, u32[]{:S(2)}, u32[]{:S(2)}) collective-permute-start(bf16[2,112,128]{2,1,0:T(8,128)(2,1)S(1)} %pad_maximum_fusion.8), channel_id=1, source_target_pairs={{2,0},{3,1},{4,2},{5,3},{6,4},{7,5},{8,6},{9,7},{10,8},{11,9},{12,... | collective-permute-start | bytes 172040 | tf_op jit(solution)/shard_map/ppermute | solution.py:15
  54.1 3.6 %collective-permute-done.9 = bf16[2,112,128]{2,1,0:T(8,128)(2,1)S(1)} collective-permute-done((bf16[2,112,128]{2,1,0:T(8,128)(2,1)S(1)}, bf16[2,112,128]{2,1,0:T(8,128)(2,1)S(1)}, u32[]{:S(2)}, u32[]{:S(2)}) %collective-permute-start.9) | collective-permute-done | bytes 57376 | tf_op jit(solution)/shard_map/ppermute | solution.py:15
  58.6 5.0 %all-gather = f32[512,128]{0,1:T(8,128)S(1)} all-gather(f32[256,128]{0,1:T(8,128)S(1)} %fusion.11), channel_id=2, replica_groups=mesh['freq'=2,'tile'=16] {'freq'}, dimensions={0}, use_global_device_ids=true | all-gather | bytes 393216 | tf_op jit(solution)/shard_map/all_gather | solution.py:137
  65.2 1.9 %collective-permute-start.11 = (bf16[2,112,128]{2,1,0:T(8,128)(2,1)S(1)}, bf16[2,112,128]{2,1,0:T(8,128)(2,1)S(1)}, u32[]{:S(2)}, u32[]{:S(2)}) collective-permute-start(bf16[2,112,128]{2,1,0:T(8,128)(2,1)S(1)} %pad_maximum_fusion.9), channel_id=1, source_target_pairs={{1,0},{2,1},{3,2},{4,3},{5,4},{6,5},{7,6},{8,7},{9,8},{10,9},{11,1... | collective-permute-start | bytes 172040 | tf_op jit(solution)/shard_map/ppermute | solution.py:15
  67.1 1.9 %collective-permute-start.10 = (bf16[1,112,128]{2,1,0:T(8,128)(2,1)S(1)}, bf16[1,112,128]{2,1,0:T(8,128)(2,1)S(1)}, u32[]{:S(2)}, u32[]{:S(2)}) collective-permute-start(bf16[1,112,128]{2,1,0:T(8,128)(2,1)S(1)} %get-tuple-element.34), channel_id=1, source_target_pairs={{4,0},{5,1},{6,2},{7,3},{8,4},{9,5},{10,6},{11,7},{12,8},{13,9},{1... | collective-permute-start | bytes 86024 | tf_op jit(solution)/shard_map/ppermute | solution.py:15
  69.1 2.5 %collective-permute-done.11 = bf16[2,112,128]{2,1,0:T(8,128)(2,1)S(1)} collective-permute-done((bf16[2,112,128]{2,1,0:T(8,128)(2,1)S(1)}, bf16[2,112,128]{2,1,0:T(8,128)(2,1)S(1)}, u32[]{:S(2)}, u32[]{:S(2)}) %collective-permute-start.11) | collective-permute-done | bytes 57376 | tf_op jit(solution)/shard_map/ppermute | solution.py:15
  71.6 1.9 %collective-permute-start.12 = (bf16[2,112,128]{2,1,0:T(8,128)(2,1)S(1)}, bf16[2,112,128]{2,1,0:T(8,128)(2,1)S(1)}, u32[]{:S(2)}, u32[]{:S(2)}) collective-permute-start(bf16[2,112,128]{2,1,0:T(8,128)(2,1)S(1)} %pad_maximum_fusion.10), channel_id=1, source_target_pairs={{2,0},{3,1},{4,2},{5,3},{6,4},{7,5},{8,6},{9,7},{10,8},{11,9},{12,... | collective-permute-start | bytes 172040 | tf_op jit(solution)/shard_map/ppermute | solution.py:15
  73.6 3.9 %collective-permute-done.12 = bf16[2,112,128]{2,1,0:T(8,128)(2,1)S(1)} collective-permute-done((bf16[2,112,128]{2,1,0:T(8,128)(2,1)S(1)}, bf16[2,112,128]{2,1,0:T(8,128)(2,1)S(1)}, u32[]{:S(2)}, u32[]{:S(2)}) %collective-permute-start.12) | collective-permute-done | bytes 57376 | tf_op jit(solution)/shard_map/ppermute | solution.py:15
  77.5 2.1 %collective-permute-start.13 = (bf16[2,112,128]{2,1,0:T(8,128)(2,1)S(1)}, bf16[2,112,128]{2,1,0:T(8,128)(2,1)S(1)}, u32[]{:S(2)}, u32[]{:S(2)}) collective-permute-start(bf16[2,112,128]{2,1,0:T(8,128)(2,1)S(1)} %pad_maximum_fusion.11), channel_id=1, source_target_pairs={{0,1},{1,2},{2,3},{3,4},{4,5},{5,6},{6,7},{7,8},{8,9},{9,10},{10,1... | collective-permute-start | bytes 172040 | tf_op jit(solution)/shard_map/ppermute | solution.py:15
  80.9 1.9 %collective-permute-start.14 = (bf16[2,112,128]{2,1,0:T(8,128)(2,1)S(1)}, bf16[2,112,128]{2,1,0:T(8,128)(2,1)S(1)}, u32[]{:S(2)}, u32[]{:S(2)}) collective-permute-start(bf16[2,112,128]{2,1,0:T(8,128)(2,1)S(1)} %pad_maximum_fusion.12), channel_id=1, source_target_pairs={{0,2},{1,3},{2,4},{3,5},{4,6},{5,7},{6,8},{7,9},{8,10},{9,11},{10,... | collective-permute-start | bytes 172040 | tf_op jit(solution)/shard_map/ppermute | solution.py:15
  82.8 3.0 %collective-permute-done.14 = bf16[2,112,128]{2,1,0:T(8,128)(2,1)S(1)} collective-permute-done((bf16[2,112,128]{2,1,0:T(8,128)(2,1)S(1)}, bf16[2,112,128]{2,1,0:T(8,128)(2,1)S(1)}, u32[]{:S(2)}, u32[]{:S(2)}) %collective-permute-start.14) | collective-permute-done | bytes 57376 | tf_op jit(solution)/shard_map/ppermute | solution.py:15
  87.7 7.2 %collective-permute-start.16 = (bf16[2,112,128]{2,1,0:T(8,128)(2,1)S(1)}, bf16[2,112,128]{2,1,0:T(8,128)(2,1)S(1)}, u32[]{:S(2)}, u32[]{:S(2)}) collective-permute-start(bf16[2,112,128]{2,1,0:T(8,128)(2,1)S(1)} %pad_maximum_fusion.13), channel_id=1, source_target_pairs={{0,1},{1,2},{2,3},{3,4},{4,5},{5,6},{6,7},{7,8},{8,9},{9,10},{10,1... | collective-permute-start | bytes 172040 | tf_op jit(solution)/shard_map/ppermute | solution.py:15
  94.9 1.9 %collective-permute-start.15 = (bf16[1,112,128]{2,1,0:T(8,128)(2,1)S(1)}, bf16[1,112,128]{2,1,0:T(8,128)(2,1)S(1)}, u32[]{:S(2)}, u32[]{:S(2)}) collective-permute-start(bf16[1,112,128]{2,1,0:T(8,128)(2,1)S(1)} %get-tuple-element.24), channel_id=1, source_target_pairs={{0,4},{1,5},{2,6},{3,7},{4,8},{5,9},{6,10},{7,11},{8,12},{9,13},{1... | collective-permute-start | bytes 86024 | tf_op jit(solution)/shard_map/ppermute | solution.py:15
  99.5 2.9 %collective-permute-done.17 = bf16[2,112,128]{2,1,0:T(8,128)(2,1)S(1)} collective-permute-done((bf16[2,112,128]{2,1,0:T(8,128)(2,1)S(1)}, bf16[2,112,128]{2,1,0:T(8,128)(2,1)S(1)}, u32[]{:S(2)}, u32[]{:S(2)}) %collective-permute-start.17) | collective-permute-done | bytes 57376 | tf_op jit(solution)/shard_map/ppermute | solution.py:15
  102.4 3.4 %collective-permute-start.18 = (bf16[2,112,128]{2,1,0:T(8,128)(2,1)S(1)}, bf16[2,112,128]{2,1,0:T(8,128)(2,1)S(1)}, u32[]{:S(2)}, u32[]{:S(2)}) collective-permute-start(bf16[2,112,128]{2,1,0:T(8,128)(2,1)S(1)} %pad_maximum_fusion.15), channel_id=1, source_target_pairs={{1,0},{2,1},{3,2},{4,3},{5,4},{6,5},{7,6},{8,7},{9,8},{10,9},{11,1... | collective-permute-start | bytes 172040 | tf_op jit(solution)/shard_map/ppermute | solution.py:15
  105.8 4.7 %collective-permute-done.18 = bf16[2,112,128]{2,1,0:T(8,128)(2,1)S(1)} collective-permute-done((bf16[2,112,128]{2,1,0:T(8,128)(2,1)S(1)}, bf16[2,112,128]{2,1,0:T(8,128)(2,1)S(1)}, u32[]{:S(2)}, u32[]{:S(2)}) %collective-permute-start.18) | collective-permute-done | bytes 57376 | tf_op jit(solution)/shard_map/ppermute | solution.py:15
  112.5 3.9 %collective-permute-done.19 = bf16[2,112,128]{2,1,0:T(8,128)(2,1)S(1)} collective-permute-done((bf16[2,112,128]{2,1,0:T(8,128)(2,1)S(1)}, bf16[2,112,128]{2,1,0:T(8,128)(2,1)S(1)}, u32[]{:S(2)}, u32[]{:S(2)}) %collective-permute-start.19) | collective-permute-done | bytes 57376 | tf_op jit(solution)/shard_map/ppermute | solution.py:15
  117.2 5.0 %all-gather.1 = f32[512,128]{0,1:T(8,128)S(1)} all-gather(f32[256,128]{0,1:T(8,128)S(1)} %fusion.6), channel_id=3, replica_groups=mesh['freq'=2,'tile'=16] {'freq'}, dimensions={0}, use_global_device_ids=true | all-gather | bytes 393216 | tf_op jit(solution)/shard_map/all_gather | solution.py:137
  (124 shorter events, 21.5 us)
Async XLA Ops:
  0.0 0.7 copy-start.3
  2.0 1.3 %copy-start.1 = (f32[1,256,128]{2,1,0:T(8,128)S(1)}, f32[1,256,128]{2,1,0:T(8,128)}, u32[]{:S(2)}) copy-start(f32[1,256,128]{2,1,0:T(8,128)} %param.7) | copy-start | bytes 393220
  3.5 5.8 %copy-start = (bf16[1,8,2,112,256]{4,3,2,1,0:T(8,128)(2,1)S(1)}, bf16[1,8,2,112,256]{4,3,2,1,0:T(8,128)(2,1)}, u32[]{:S(2)}) copy-start(bf16[1,8,2,112,256]{4,3,2,1,0:T(8,128)(2,1)} %param.10) | copy-start | bytes 2752516
  4.0 10.5 %collective-permute-start = (bf16[1,112,128]{2,1,0:T(8,128)(2,1)S(1)}, bf16[1,112,128]{2,1,0:T(8,128)(2,1)S(1)}, u32[]{:S(2)}, u32[]{:S(2)}) collective-permute-start(bf16[1,112,128]{2,1,0:T(8,128)(2,1)S(1)} %get-tuple-element.54), channel_id=1, source_target_pairs={{4,0},{5,1},{6,2},{7,3},{8,4},{9,5},{10,6},{11,7},{12,8},{13,9},{1... | collective-permute-start | bytes 86024 | tf_op jit(solution)/shard_map/ppermute | solution.py:15
  6.2 6.4 %collective-permute-start.1 = (bf16[2,112,128]{2,1,0:T(8,128)(2,1)S(1)}, bf16[2,112,128]{2,1,0:T(8,128)(2,1)S(1)}, u32[]{:S(2)}, u32[]{:S(2)}) collective-permute-start(bf16[2,112,128]{2,1,0:T(8,128)(2,1)S(1)} %pad_maximum_fusion.1), channel_id=1, source_target_pairs={{1,0},{2,1},{3,2},{4,3},{5,4},{6,5},{7,6},{8,7},{9,8},{10,9},{11,1... | collective-permute-start | bytes 172040 | tf_op jit(solution)/shard_map/ppermute | solution.py:15
  9.3 0.7 copy-start.4
  12.6 5.8 %collective-permute-start.2 = (bf16[2,112,128]{2,1,0:T(8,128)(2,1)S(1)}, bf16[2,112,128]{2,1,0:T(8,128)(2,1)S(1)}, u32[]{:S(2)}, u32[]{:S(2)}) collective-permute-start(bf16[2,112,128]{2,1,0:T(8,128)(2,1)S(1)} %pad_maximum_fusion.2), channel_id=1, source_target_pairs={{2,0},{3,1},{4,2},{5,3},{6,4},{7,5},{8,6},{9,7},{10,8},{11,9},{12,... | collective-permute-start | bytes 172040 | tf_op jit(solution)/shard_map/ppermute | solution.py:15
  18.4 2.7 %copy-start.2 = (bf16[1,256,128]{2,1,0:T(8,128)(2,1)S(1)}, bf16[1,256,128]{2,1,0:T(8,128)(2,1)}, u32[]{:S(2)}) copy-start(bf16[1,256,128]{2,1,0:T(8,128)(2,1)} %param.8) | copy-start | bytes 196612
  18.5 3.8 %collective-permute-start.3 = (bf16[2,112,128]{2,1,0:T(8,128)(2,1)S(1)}, bf16[2,112,128]{2,1,0:T(8,128)(2,1)S(1)}, u32[]{:S(2)}, u32[]{:S(2)}) collective-permute-start(bf16[2,112,128]{2,1,0:T(8,128)(2,1)S(1)} %pad_maximum_fusion.3), channel_id=1, source_target_pairs={{0,1},{1,2},{2,3},{3,4},{4,5},{5,6},{6,7},{7,8},{8,9},{9,10},{10,1... | collective-permute-start | bytes 172040 | tf_op jit(solution)/shard_map/ppermute | solution.py:15
  22.3 4.9 %collective-permute-start.4 = (bf16[2,112,128]{2,1,0:T(8,128)(2,1)S(1)}, bf16[2,112,128]{2,1,0:T(8,128)(2,1)S(1)}, u32[]{:S(2)}, u32[]{:S(2)}) collective-permute-start(bf16[2,112,128]{2,1,0:T(8,128)(2,1)S(1)} %pad_maximum_fusion.4), channel_id=1, source_target_pairs={{0,2},{1,3},{2,4},{3,5},{4,6},{5,7},{6,8},{7,9},{8,10},{9,11},{10,... | collective-permute-start | bytes 172040 | tf_op jit(solution)/shard_map/ppermute | solution.py:15
  29.1 9.2 %collective-permute-start.6 = (bf16[2,112,128]{2,1,0:T(8,128)(2,1)S(1)}, bf16[2,112,128]{2,1,0:T(8,128)(2,1)S(1)}, u32[]{:S(2)}, u32[]{:S(2)}) collective-permute-start(bf16[2,112,128]{2,1,0:T(8,128)(2,1)S(1)} %pad_maximum_fusion.5), channel_id=1, source_target_pairs={{0,1},{1,2},{2,3},{3,4},{4,5},{5,6},{6,7},{7,8},{8,9},{9,10},{10,1... | collective-permute-start | bytes 172040 | tf_op jit(solution)/shard_map/ppermute | solution.py:15
  36.3 4.6 %collective-permute-start.5 = (bf16[1,112,128]{2,1,0:T(8,128)(2,1)S(1)}, bf16[1,112,128]{2,1,0:T(8,128)(2,1)S(1)}, u32[]{:S(2)}, u32[]{:S(2)}) collective-permute-start(bf16[1,112,128]{2,1,0:T(8,128)(2,1)S(1)} %get-tuple-element.44), channel_id=1, source_target_pairs={{0,4},{1,5},{2,6},{3,7},{4,8},{5,9},{6,10},{7,11},{8,12},{9,13},{1... | collective-permute-start | bytes 86024 | tf_op jit(solution)/shard_map/ppermute | solution.py:15
  38.3 5.8 %collective-permute-start.7 = (bf16[2,112,128]{2,1,0:T(8,128)(2,1)S(1)}, bf16[2,112,128]{2,1,0:T(8,128)(2,1)S(1)}, u32[]{:S(2)}, u32[]{:S(2)}) collective-permute-start(bf16[2,112,128]{2,1,0:T(8,128)(2,1)S(1)} %pad_maximum_fusion.6), channel_id=1, source_target_pairs={{0,2},{1,3},{2,4},{3,5},{4,6},{5,7},{6,8},{7,9},{8,10},{9,11},{10,... | collective-permute-start | bytes 172040 | tf_op jit(solution)/shard_map/ppermute | solution.py:15
  44.2 7.7 %collective-permute-start.8 = (bf16[2,112,128]{2,1,0:T(8,128)(2,1)S(1)}, bf16[2,112,128]{2,1,0:T(8,128)(2,1)S(1)}, u32[]{:S(2)}, u32[]{:S(2)}) collective-permute-start(bf16[2,112,128]{2,1,0:T(8,128)(2,1)S(1)} %pad_maximum_fusion.7), channel_id=1, source_target_pairs={{1,0},{2,1},{3,2},{4,3},{5,4},{6,5},{7,6},{8,7},{9,8},{10,9},{11,1... | collective-permute-start | bytes 172040 | tf_op jit(solution)/shard_map/ppermute | solution.py:15
  51.9 5.8 %collective-permute-start.9 = (bf16[2,112,128]{2,1,0:T(8,128)(2,1)S(1)}, bf16[2,112,128]{2,1,0:T(8,128)(2,1)S(1)}, u32[]{:S(2)}, u32[]{:S(2)}) collective-permute-start(bf16[2,112,128]{2,1,0:T(8,128)(2,1)S(1)} %pad_maximum_fusion.8), channel_id=1, source_target_pairs={{2,0},{3,1},{4,2},{5,3},{6,4},{7,5},{8,6},{9,7},{10,8},{11,9},{12,... | collective-permute-start | bytes 172040 | tf_op jit(solution)/shard_map/ppermute | solution.py:15
  65.2 6.4 %collective-permute-start.11 = (bf16[2,112,128]{2,1,0:T(8,128)(2,1)S(1)}, bf16[2,112,128]{2,1,0:T(8,128)(2,1)S(1)}, u32[]{:S(2)}, u32[]{:S(2)}) collective-permute-start(bf16[2,112,128]{2,1,0:T(8,128)(2,1)S(1)} %pad_maximum_fusion.9), channel_id=1, source_target_pairs={{1,0},{2,1},{3,2},{4,3},{5,4},{6,5},{7,6},{8,7},{9,8},{10,9},{11,1... | collective-permute-start | bytes 172040 | tf_op jit(solution)/shard_map/ppermute | solution.py:15
  67.1 6.4 %collective-permute-start.10 = (bf16[1,112,128]{2,1,0:T(8,128)(2,1)S(1)}, bf16[1,112,128]{2,1,0:T(8,128)(2,1)S(1)}, u32[]{:S(2)}, u32[]{:S(2)}) collective-permute-start(bf16[1,112,128]{2,1,0:T(8,128)(2,1)S(1)} %get-tuple-element.34), channel_id=1, source_target_pairs={{4,0},{5,1},{6,2},{7,3},{8,4},{9,5},{10,6},{11,7},{12,8},{13,9},{1... | collective-permute-start | bytes 86024 | tf_op jit(solution)/shard_map/ppermute | solution.py:15
  71.6 5.8 %collective-permute-start.12 = (bf16[2,112,128]{2,1,0:T(8,128)(2,1)S(1)}, bf16[2,112,128]{2,1,0:T(8,128)(2,1)S(1)}, u32[]{:S(2)}, u32[]{:S(2)}) collective-permute-start(bf16[2,112,128]{2,1,0:T(8,128)(2,1)S(1)} %pad_maximum_fusion.10), channel_id=1, source_target_pairs={{2,0},{3,1},{4,2},{5,3},{6,4},{7,5},{8,6},{9,7},{10,8},{11,9},{12,... | collective-permute-start | bytes 172040 | tf_op jit(solution)/shard_map/ppermute | solution.py:15
  77.5 3.4 %collective-permute-start.13 = (bf16[2,112,128]{2,1,0:T(8,128)(2,1)S(1)}, bf16[2,112,128]{2,1,0:T(8,128)(2,1)S(1)}, u32[]{:S(2)}, u32[]{:S(2)}) collective-permute-start(bf16[2,112,128]{2,1,0:T(8,128)(2,1)S(1)} %pad_maximum_fusion.11), channel_id=1, source_target_pairs={{0,1},{1,2},{2,3},{3,4},{4,5},{5,6},{6,7},{7,8},{8,9},{9,10},{10,1... | collective-permute-start | bytes 172040 | tf_op jit(solution)/shard_map/ppermute | solution.py:15
  80.9 4.9 %collective-permute-start.14 = (bf16[2,112,128]{2,1,0:T(8,128)(2,1)S(1)}, bf16[2,112,128]{2,1,0:T(8,128)(2,1)S(1)}, u32[]{:S(2)}, u32[]{:S(2)}) collective-permute-start(bf16[2,112,128]{2,1,0:T(8,128)(2,1)S(1)} %pad_maximum_fusion.12), channel_id=1, source_target_pairs={{0,2},{1,3},{2,4},{3,5},{4,6},{5,7},{6,8},{7,9},{8,10},{9,11},{10,... | collective-permute-start | bytes 172040 | tf_op jit(solution)/shard_map/ppermute | solution.py:15
  87.7 9.1 %collective-permute-start.16 = (bf16[2,112,128]{2,1,0:T(8,128)(2,1)S(1)}, bf16[2,112,128]{2,1,0:T(8,128)(2,1)S(1)}, u32[]{:S(2)}, u32[]{:S(2)}) collective-permute-start(bf16[2,112,128]{2,1,0:T(8,128)(2,1)S(1)} %pad_maximum_fusion.13), channel_id=1, source_target_pairs={{0,1},{1,2},{2,3},{3,4},{4,5},{5,6},{6,7},{7,8},{8,9},{9,10},{10,1... | collective-permute-start | bytes 172040 | tf_op jit(solution)/shard_map/ppermute | solution.py:15
  94.9 4.6 %collective-permute-start.15 = (bf16[1,112,128]{2,1,0:T(8,128)(2,1)S(1)}, bf16[1,112,128]{2,1,0:T(8,128)(2,1)S(1)}, u32[]{:S(2)}, u32[]{:S(2)}) collective-permute-start(bf16[1,112,128]{2,1,0:T(8,128)(2,1)S(1)} %get-tuple-element.24), channel_id=1, source_target_pairs={{0,4},{1,5},{2,6},{3,7},{4,8},{5,9},{6,10},{7,11},{8,12},{9,13},{1... | collective-permute-start | bytes 86024 | tf_op jit(solution)/shard_map/ppermute | solution.py:15
  96.9 5.5 %collective-permute-start.17 = (bf16[2,112,128]{2,1,0:T(8,128)(2,1)S(1)}, bf16[2,112,128]{2,1,0:T(8,128)(2,1)S(1)}, u32[]{:S(2)}, u32[]{:S(2)}) collective-permute-start(bf16[2,112,128]{2,1,0:T(8,128)(2,1)S(1)} %pad_maximum_fusion.14), channel_id=1, source_target_pairs={{0,2},{1,3},{2,4},{3,5},{4,6},{5,7},{6,8},{7,9},{8,10},{9,11},{10,... | collective-permute-start | bytes 172040 | tf_op jit(solution)/shard_map/ppermute | solution.py:15
  102.4 8.1 %collective-permute-start.18 = (bf16[2,112,128]{2,1,0:T(8,128)(2,1)S(1)}, bf16[2,112,128]{2,1,0:T(8,128)(2,1)S(1)}, u32[]{:S(2)}, u32[]{:S(2)}) collective-permute-start(bf16[2,112,128]{2,1,0:T(8,128)(2,1)S(1)} %pad_maximum_fusion.15), channel_id=1, source_target_pairs={{1,0},{2,1},{3,2},{4,3},{5,4},{6,5},{7,6},{8,7},{9,8},{10,9},{11,1... | collective-permute-start | bytes 172040 | tf_op jit(solution)/shard_map/ppermute | solution.py:15
  110.5 5.8 %collective-permute-start.19 = (bf16[2,112,128]{2,1,0:T(8,128)(2,1)S(1)}, bf16[2,112,128]{2,1,0:T(8,128)(2,1)S(1)}, u32[]{:S(2)}, u32[]{:S(2)}) collective-permute-start(bf16[2,112,128]{2,1,0:T(8,128)(2,1)S(1)} %pad_maximum_fusion.16), channel_id=1, source_target_pairs={{2,0},{3,1},{4,2},{5,3},{6,4},{7,5},{8,6},{9,7},{10,8},{11,9},{12,... | collective-permute-start | bytes 172040 | tf_op jit(solution)/shard_map/ppermute | solution.py:15
where the time goes:
time: 124 us
  starting transfers between devices  53.5 us (43%)
  waiting for transfers between devices  44.7 us (36%)
  blocking collectives  9.91 us (8%)
  local copies, waits for them, and re-layouts  6.09 us (5%)
  matrix products  4.85 us (4%)
  other arithmetic  2.94 us (2%)
  between operations  1.45 us (1%)
    ppermute x20, starting transfers between devices, shifted(): lax.ppermute(value, axis, [(source, source + steps) for source in range(l...  53.5 us
    ppermute x20, waiting for transfers between devices, shifted(): lax.ppermute(value, axis, [(source, source + steps) for source in range(l...  44.7 us
    all_gather x2, blocking collectives, on_device(): lax.all_gather(updated[None], 'freq', axis=0, tiled=True)  9.91 us
    dot_general x8, matrix products, left_dot(): lax.dot_general(factor, values, (((0,), (0,)), ((), ())), preferred_eleme...  2.55 us
    unnamed x24, local copies, waits for them, and re-layouts  2.53 us
  transfers between devices with their start and end apart: 20, of which 16 were waited for; matrix products, arithmetic and copies ran while one was open for 1% of the time, Pallas kernels for 0%

commit v1 on v0

v1 whole, which is shorter than its diff:
```python
import math

import jax
import jax.numpy as jnp
from jax import lax
from jax.experimental import pallas as pl
from jax.experimental.pallas import tpu as pltpu
from jax.sharding import PartitionSpec as P

NT = 2048
ITERS = 2
F32 = jnp.float32
BF16 = jnp.bfloat16


def slot_order(slots):
    center = slots // 2
    offsets = [s - center for s in range(slots)]
    key = {2: 0, 1: 1, 3: 2}
    far = sorted((o for o in offsets if o), key=lambda o: (key.get(abs(o), 3), abs(o), o))
    return far + [0]


def make_kernel(ntile, nfreq, slots, levels, rows, width):
    center = slots // 2
    half = width // 2
    order = slot_order(slots)

    def quarter_turn(sign):
        lane = lax.broadcasted_iota(jnp.int32, (1, width), 1)
        return jnp.where(lane < half, -sign, sign).astype(F32)

    def kernel(
        model_hbm, data_hbm, v_hbm, u_hbm, ranks, window, stepping,
        out,
        model_ref, data_ref, v, u, vt, ut, z_ref,
        fsent, fgot, asent, agot, zsent, zgot,
        local_sem, v_sem, u_sem, send_sem, recv_sem, zsend_sem, zrecv_sem,
    ):
        me = lax.axis_index("tile")
        freq = lax.axis_index("freq")

        def inside(index):
            return jnp.logical_and(index >= 0, index < ntile)

        load_model = pltpu.make_async_copy(model_hbm, model_ref, local_sem.at[0])
        load_data = pltpu.make_async_copy(data_hbm, data_ref, local_sem.at[1])
        load_v = [pltpu.make_async_copy(v_hbm.at[s], v.at[s], v_sem.at[s]) for s in range(slots)]
        load_u = [pltpu.make_async_copy(u_hbm.at[s], u.at[s], u_sem.at[s]) for s in range(slots)]
        load_model.start()
        for off in order:
            load_v[center + off].start()
        for off in order:
            load_u[center + off].start()
        load_data.start()

        barrier = pltpu.get_barrier_semaphore()
        expected = jnp.int32(nfreq - 1)
        for off in range(-center, center + 1):
            if off == 0:
                continue
            there = inside(me + off)

            @pl.when(there)
            def _():
                pl.semaphore_signal(barrier, inc=1, device_id={"tile": me + off})

            expected = expected + there.astype(jnp.int32)
        for other in range(1, nfreq):
            pl.semaphore_signal(barrier, inc=1, device_id={"freq": lax.rem(freq + other, nfreq)})

        for off in order:
            if off == 0:
                continue

            @pl.when(jnp.logical_not(inside(me - off)))
            def _():
                for step in range(ITERS):
                    fgot[step, center + off] = jnp.zeros((levels, width), BF16)

            @pl.when(jnp.logical_not(inside(me + off)))
            def _():
                for step in range(ITERS):
                    agot[step, center + off] = jnp.zeros((levels, width), BF16)

        plus = quarter_turn(1.0)
        minus = quarter_turn(-1.0)

        def rotated(value, sign_row):
            return (pltpu.roll(value, half, 1) * sign_row).astype(BF16)

        level_ids = lax.broadcasted_iota(jnp.int32, (levels, width), 0)

        def hop(src, dst, phase, step, s, target):
            return pltpu.make_async_remote_copy(
                src_ref=src.at[step, s], dst_ref=dst.at[step, s],
                send_sem=send_sem.at[step, phase, s], recv_sem=recv_sem.at[step, phase, s],
                device_id={"tile": target}, device_id_type=pl.DeviceIdType.MESH,
            )

        def freq_copy(step, other):
            return pltpu.make_async_remote_copy(
                src_ref=zsent.at[step], dst_ref=zgot.at[step, other - 1],
                send_sem=zsend_sem.at[step, other - 1], recv_sem=zrecv_sem.at[step, other - 1],
                device_id={"freq": lax.rem(freq + other, nfreq)},
                device_id_type=pl.DeviceIdType.MESH,
            )

        load_model.wait()
        model = model_ref[...]
        for step in range(ITERS):
            xb = model.astype(BF16)
            rx = rotated(xb.astype(F32), plus)
            for place, off in enumerate(order):
                s = center + off
                if step == 0:
                    load_v[s].wait()
                coef = jnp.dot(v[s, 0], xb, preferred_element_type=F32) + jnp.dot(
                    v[s, 1], rx, preferred_element_type=F32
                )
                coef = jnp.where(level_ids < ranks[me, s], coef, 0.0).astype(BF16)
                if off == 0:
                    fgot[step, s] = coef
                    continue
                fsent[step, s] = coef
                if step == 0 and place == 0:
                    pl.semaphore_wait(barrier, expected)

                @pl.when(inside(me + off))
                def _():
                    hop(fsent, fgot, 0, step, s, me + off).start()

            if step == 0:
                for off in order:
                    s = center + off
                    load_u[s].wait()
                    ut[s] = jnp.transpose(u[s].reshape(2 * levels, rows))
                load_data.wait()
            image = -data_ref[...].astype(F32)
            for off in [0] + order[:-1]:
                s = center + off
                if off != 0:

                    @pl.when(inside(me - off))
                    def _():
                        hop(fsent, fgot, 0, step, s, me).wait_recv()

                c = fgot[step, s]
                rc = rotated(c.astype(F32), plus)
                image = image + jnp.dot(
                    ut[s], jnp.concatenate([c, rc], axis=0), preferred_element_type=F32
                )
            resid = image.astype(BF16)
            rr = rotated(resid.astype(F32), minus)
            for off in order:
                s = center + off
                back = jnp.dot(u[s, 0], resid, preferred_element_type=F32) + jnp.dot(
                    u[s, 1], rr, preferred_element_type=F32
                )
                rank = ranks[jnp.clip(me - off, 0, ntile - 1), s]
                back = jnp.where(level_ids < rank, back, 0.0).astype(BF16)
                if off == 0:
                    agot[step, s] = back
                    continue
                asent[step, s] = back

                @pl.when(inside(me - off))
                def _():
                    hop(asent, agot, 1, step, s, me - off).start()

            if step == 0:
                for off in order:
                    s = center + off
                    vt[s] = jnp.transpose(v[s].reshape(2 * levels, rows))
                wf = window[...].astype(F32)
                ends = []
                for column in range(2):
                    wide = jnp.broadcast_to(wf[:, column:column + 1], (half, width))
                    wide = jnp.concatenate([wide, wide], axis=0)
                    ends.append(jnp.transpose(wide)[0:8])
                span = ends[1] - ends[0]
                own_gate = (span / NT)[0:1]
                gates = []
                for other in range(1, nfreq):
                    source = lax.rem(freq + nfreq - other, nfreq)
                    delta = (freq - source).astype(F32)
                    turn = delta * (ends[0] + ends[1] - 1.0)
                    turn = turn - (2 * NT) * jnp.floor(turn / (2 * NT))
                    phase = turn * (math.pi / NT)
                    theta = jnp.full_like(span, math.pi / NT) * delta
                    mag = jnp.sin(theta * span) / (NT * jnp.sin(theta))
                    gates.append(((mag * jnp.cos(phase))[0:1], (mag * jnp.sin(phase))[0:1] * plus))
            grad = jnp.zeros((rows, width), F32)
            for off in [0] + order[:-1]:
                s = center + off
                if off != 0:

                    @pl.when(inside(me + off))
                    def _():
                        hop(asent, agot, 1, step, s, me).wait_recv()

                b = agot[step, s]
                rb = rotated(b.astype(F32), minus)
                grad = grad + jnp.dot(
                    vt[s], jnp.concatenate([b, rb], axis=0), preferred_element_type=F32
                )
            z = model - stepping[0] * grad
            zsent[step] = z.astype(BF16)
            for other in range(1, nfreq):
                freq_copy(step, other).start()
            model = own_gate * z
            for other in range(1, nfreq):
                freq_copy(step, other).wait_recv()
                zg = zgot[step, other - 1].astype(F32)
                gre, gim = gates[other - 1]
                model = model + gre * zg + gim * pltpu.roll(zg, half, 1)
        out[...] = model

        for step in range(ITERS):
            for other in range(1, nfreq):
                freq_copy(step, other).wait_send()
            for off in order[:-1]:
                s = center + off

                @pl.when(inside(me + off))
                def _():
                    hop(fsent, fgot, 0, step, s, me).wait_send()

                @pl.when(inside(me - off))
                def _():
                    hop(asent, agot, 1, step, s, me).wait_send()

    return kernel


def on_device(model_start, data, col_factors, row_factors, ranks, gate_window, step_sizes):
    ntile = lax.axis_size("tile")
    nfreq = lax.axis_size("freq")
    slots, _, levels, rows = col_factors.shape[1:]
    width = model_start.shape[-1]
    any_space = pl.BlockSpec(memory_space=pl.ANY)
    vmem = pl.BlockSpec(memory_space=pltpu.VMEM)
    smem = pl.BlockSpec(memory_space=pltpu.SMEM)
    block = (ITERS, slots, levels, width)
    peers = max(nfreq - 1, 1)
    result = pl.pallas_call(
        make_kernel(ntile, nfreq, slots, levels, rows, width),
        name="gradient_steps",
        out_shape=jax.ShapeDtypeStruct((rows, width), F32),
        in_specs=[any_space, any_space, any_space, any_space, smem, vmem, smem],
        out_specs=vmem,
        scratch_shapes=[
            pltpu.VMEM((rows, width), F32),
            pltpu.VMEM((rows, width), BF16),
            pltpu.VMEM((slots, 2, levels, rows), BF16),
            pltpu.VMEM((slots, 2, levels, rows), BF16),
            pltpu.VMEM((slots, rows, 2 * levels), BF16),
            pltpu.VMEM((slots, rows, 2 * levels), BF16),
            pltpu.VMEM((rows, width), F32),
            pltpu.VMEM(block, BF16),
            pltpu.VMEM(block, BF16),
            pltpu.VMEM(block, BF16),
            pltpu.VMEM(block, BF16),
            pltpu.VMEM((ITERS, rows, width), BF16),
            pltpu.VMEM((ITERS, peers, rows, width), BF16),
            pltpu.SemaphoreType.DMA((2,)),
            pltpu.SemaphoreType.DMA((slots,)),
            pltpu.SemaphoreType.DMA((slots,)),
            pltpu.SemaphoreType.DMA((ITERS, 2, slots)),
            pltpu.SemaphoreType.DMA((ITERS, 2, slots)),
            pltpu.SemaphoreType.DMA((ITERS, peers)),
            pltpu.SemaphoreType.DMA((ITERS, peers)),
        ],
        compiler_params=pltpu.CompilerParams(collective_id=0, has_side_effects=True),
    )(model_start[0], data[0], col_factors[0], row_factors[0], ranks[0], gate_window, step_sizes)
    return result[None]


def solution(mesh):
    return jax.shard_map(
        on_device,
        mesh=mesh,
        in_specs=(
            P("freq", "tile", None),
            P("freq", "tile", None),
            P("freq", "tile", None, None, None),
            P("freq", "tile", None, None, None),
            P("freq", None, None),
            P(),
            P("freq"),
        ),
        out_specs=P("freq", "tile", None),
        check_vma=False,
    )
```

time: 124 us -> 37.7 us (0.30)
  the two profiles are of different devices: /device:TPU:23 before, /device:TPU:0 now
where the time goes in v1:
time: 37.7 us; the launch traced here: 37.4 us
  Pallas kernels  33.1 us (88%)
  local copies, waits for them, and re-layouts  3.63 us (10%)
  between operations  0.67 us (2%)
    pallas_call x1, Pallas kernels, on_device(): pl.pallas_call(make_kernel(ntile, nfreq, slots, levels, rows, width), nam...  33.1 us
    unnamed x6, local copies, waits for them, and re-layouts  2.97 us

profile of v1, /device:TPU:0, one launch (start us, length us, event | category | flops | bytes accessed | tf_op | source)
XLA Modules:
  0.0 37.4 jit_solution(15519508243988638595)
XLA Ops:
  0.7 0.0 copy-start
  0.7 0.7 %copy-done = s32[1,16,8]{1,2,0:T(8,128)S(1)} copy-done((s32[1,16,8]{1,2,0:T(8,128)S(1)}, s32[1,16,8]{1,2,0:T(8,128)}, u32[]{:S(2)}) %copy-start) | copy-done | bytes 536
  1.3 0.0 copy-start.1
  1.3 0.7 %copy.8.ranks = s32[16,8]{1,0:T(8,128)} copy(s32[16,8]{0,1:T(8,128)S(1)} %bitcast.11) | data formatting | bytes 1024 | tf_op jit(solution)/shard_map/squeeze | solution.py:275
  2.0 0.0 copy-done.1
  2.0 0.7 %copy.9.window = s32[64,2]{1,0:T(8,128)} copy(s32[64,2]{0,1:T(2,128)S(1)} %copy-done.1) | data formatting | bytes 1024 | tf_op args[5]
  2.7 33.1 %gradient_steps.1 = f32[256,128]{1,0:T(8,128)} custom-call(f32[256,128]{1,0:T(8,128)} %bitcast.9, bf16[256,128]{1,0:T(8,128)(2,1)} %bitcast.10, bf16[8,2,112,256]{3,2,1,0:T(8,128)(2,1)} %bitcast.6, bf16[8,2,112,256]{3,2,1,0:T(8,128)(2,1)} %bitcast.7, s32[16,8]{1,0:T(8,128)} %copy.8.ranks, s32[64,2]{1,0:T(8,128)} %copy.9.window, f32[1]{0:T(128)S(6)} %copy.11.stepping), custom_call_target="tpu_custom_call" | custom-call | tf_op jit(solution)/shard_map/gradient_steps/pallas_call | solution.py:246
  35.9 1.6 %copy.12 = f32[1,256,128]{2,1,0:T(8,128)} copy(f32[1,256,128]{2,1,0:T(8,128)} %bitcast.8) | data formatting | bytes 262144
Async XLA Ops:
  0.7 0.7 %copy-start = (s32[1,16,8]{1,2,0:T(8,128)S(1)}, s32[1,16,8]{1,2,0:T(8,128)}, u32[]{:S(2)}) copy-start(s32[1,16,8]{1,2,0:T(8,128)} %param.11) | copy-start | bytes 1540
  1.3 0.7 %copy-start.1 = (s32[64,2]{0,1:T(2,128)S(1)}, s32[64,2]{0,1:T(2,128)}, u32[]{:S(2)}) copy-start(s32[64,2]{0,1:T(2,128)} %param.12) | copy-start | bytes 1540

commit v2 on v1

v2 whole, which is shorter than its diff:
```python
import math

import jax
import jax.numpy as jnp
from jax import lax
from jax.experimental import pallas as pl
from jax.experimental.pallas import tpu as pltpu
from jax.sharding import PartitionSpec as P

NT = 2048
ITERS = 2
F32 = jnp.float32
BF16 = jnp.bfloat16
GROUPS = 4
ZPARTS = 2
RECEIVE = (0, 1, 2, 3)


def slot_order(slots):
    center = slots // 2
    offsets = [s - center for s in range(slots)]
    key = {2: 0, 3: 1, 1: 2}
    far = sorted((o for o in offsets if o), key=lambda o: (key.get(abs(o), 3), abs(o), -o))
    return far + [0]


def make_kernel(ntile, nfreq, slots, levels, rows, width):
    center = slots // 2
    half = width // 2
    order = slot_order(slots)
    per_group = slots // GROUPS
    groups = [list(range(g * per_group, (g + 1) * per_group)) for g in range(GROUPS)]
    group_rows = per_group * levels

    def kernel(
        model_hbm, data_hbm, v_hbm, u_hbm, ranks_hbm, window_hbm, stepping_hbm,
        out,
        ranks, window, stepping, model_ref, data_ref, v, u, vt, ut,
        fsent, fgot, asent, agot, zsent, zgot,
        local_sem, v_sem, u_sem, send_sem, recv_sem, zsend_sem, zrecv_sem,
    ):
        me = lax.axis_index("tile")
        freq = lax.axis_index("freq")

        def inside(index):
            return jnp.logical_and(index >= 0, index < ntile)

        def at(place):
            return pl.ds(place * levels, levels)

        def loads(hbm, ref, sem):
            return [
                pltpu.make_async_copy(
                    hbm.at[center + off, part],
                    ref.at[at(place), pl.ds(part * rows, rows)],
                    sem.at[place, part],
                )
                for place, off in enumerate(order)
                for part in range(2)
            ]

        load_model = pltpu.make_async_copy(model_hbm, model_ref, local_sem.at[0])
        load_data = pltpu.make_async_copy(data_hbm, data_ref, local_sem.at[1])
        load_ranks = pltpu.make_async_copy(ranks_hbm, ranks, local_sem.at[2])
        load_window = pltpu.make_async_copy(window_hbm, window, local_sem.at[3])
        load_step = pltpu.make_async_copy(stepping_hbm, stepping, local_sem.at[4])
        load_v = loads(v_hbm, v, v_sem)
        load_u = loads(u_hbm, u, u_sem)

        barrier = pltpu.get_barrier_semaphore()
        expected = jnp.int32(nfreq - 1)
        for off in range(-center, center + 1):
            if off == 0:
                continue
            there = inside(me + off)

            @pl.when(there)
            def _():
                pl.semaphore_signal(barrier, inc=1, device_id={"tile": me + off})

            expected = expected + there.astype(jnp.int32)
        for other in range(1, nfreq):
            pl.semaphore_signal(barrier, inc=1, device_id={"freq": lax.rem(freq + other, nfreq)})
        for copy in [load_model, load_ranks] + load_v + load_u + [load_data, load_window, load_step]:
            copy.start()

        for place, off in enumerate(order):
            if off == 0:
                continue

            @pl.when(jnp.logical_not(inside(me - off)))
            def _():
                for step in range(ITERS):
                    fgot[step, at(place)] = jnp.zeros((levels, width), BF16)

            @pl.when(jnp.logical_not(inside(me + off)))
            def _():
                for step in range(ITERS):
                    agot[step, at(place)] = jnp.zeros((levels, width), BF16)

        lane = lax.broadcasted_iota(jnp.int32, (1, width), 1)
        plus = jnp.where(lane < half, -1.0, 1.0).astype(F32)

        def turned(value):
            return pltpu.roll(value, half, 1) * plus

        level_ids = lax.broadcasted_iota(jnp.int32, (levels, width), 0)

        def hop(src, dst, phase, step, place, target):
            return pltpu.make_async_remote_copy(
                src_ref=src.at[step, at(place)], dst_ref=dst.at[step, at(place)],
                send_sem=send_sem.at[step, phase, place],
                recv_sem=recv_sem.at[step, phase, place],
                device_id={"tile": target}, device_id_type=pl.DeviceIdType.MESH,
            )

        def freq_copy(step, other, part):
            where = pl.ds(part * (rows // ZPARTS), rows // ZPARTS)
            return pltpu.make_async_remote_copy(
                src_ref=zsent.at[step, where], dst_ref=zgot.at[step, other - 1, where],
                send_sem=zsend_sem.at[step, other - 1, part],
                recv_sem=zrecv_sem.at[step, other - 1, part],
                device_id={"freq": lax.rem(freq + other, nfreq)},
                device_id_type=pl.DeviceIdType.MESH,
            )

        def spread(factor, values, sent, got, phase, step, heading, before):
            for g, places in enumerate(groups):
                before(g)
                block = jnp.dot(
                    factor[pl.ds(g * group_rows, group_rows)], values,
                    preferred_element_type=F32,
                )
                for index, place in enumerate(places):
                    off = order[place]
                    column = me if phase == 0 else jnp.clip(me - off, 0, ntile - 1)
                    part = block[index * levels:(index + 1) * levels]
                    part = jnp.where(level_ids < ranks[center + off, column], part, 0.0)
                    target = got if off == 0 else sent
                    target[step, at(place)] = part.astype(BF16)
                if phase == 0 and step == 0 and g == 0:
                    pl.semaphore_wait(barrier, expected)
                for place in places:
                    off = heading * order[place]
                    if off == 0:
                        continue

                    @pl.when(inside(me + off))
                    def _():
                        hop(sent, got, phase, step, place, me + off).start()

        def collect(turned_factor, sent, got, phase, step, heading, parts):
            size = rows // parts
            totals = [jnp.zeros((size, width), F32) for _ in range(2 * parts)]
            for g in RECEIVE:
                for place in groups[g]:
                    off = heading * order[place]
                    if off == 0:
                        continue

                    @pl.when(inside(me - off))
                    def _():
                        hop(sent, got, phase, step, place, me).wait_recv()

                values = got[step, pl.ds(g * group_rows, group_rows)]
                for part in range(parts):
                    for side in range(2):
                        start = side * rows + part * size
                        totals[2 * part + side] += jnp.dot(
                            turned_factor[g, pl.ds(start, size)], values,
                            preferred_element_type=F32,
                        )
                    if g == RECEIVE[-1]:
                        yield part, totals[2 * part], turned(totals[2 * part + 1])

        def no_wait(g):
            return None

        def wait_v(g):
            for place in groups[g]:
                for part in range(2):
                    load_v[2 * place + part].wait()

        load_model.wait()
        load_ranks.wait()
        model = model_ref[...]
        for step in range(ITERS):
            xb = model.astype(BF16)
            xx = jnp.concatenate([xb, turned(xb.astype(F32)).astype(BF16)], axis=0)
            spread(v, xx, fsent, fgot, 0, step, 1, wait_v if step == 0 else no_wait)
            if step == 0:
                for g, places in enumerate(groups):
                    for place in places:
                        for part in range(2):
                            load_u[2 * place + part].wait()
                    ut[g] = jnp.transpose(u[pl.ds(g * group_rows, group_rows)])
                load_data.wait()
            (_, direct, crossed), = collect(ut, fsent, fgot, 0, step, 1, 1)
            resid = (direct + crossed - data_ref[...].astype(F32)).astype(BF16)
            rr = jnp.concatenate([resid, (-turned(resid.astype(F32))).astype(BF16)], axis=0)
            spread(u, rr, asent, agot, 1, step, -1, no_wait)
            if step == 0:
                for g in range(GROUPS):
                    vt[g] = jnp.transpose(v[pl.ds(g * group_rows, group_rows)])
                load_window.wait()
                load_step.wait()
                wf = window[...].astype(F32)
                ends = [
                    jnp.broadcast_to(
                        jnp.concatenate([wf[row:row + 1]] * 2, axis=1), (8, width)
                    )
                    for row in range(2)
                ]
                span = ends[1] - ends[0]
                own_gate = (span / NT)[0:1]
                gates = []
                for other in range(1, nfreq):
                    source = lax.rem(freq + nfreq - other, nfreq)
                    delta = (freq - source).astype(F32)
                    turn = delta * (ends[0] + ends[1] - 1.0)
                    turn = turn - (2 * NT) * jnp.floor(turn / (2 * NT))
                    phase = turn * (math.pi / NT)
                    theta = jnp.full_like(span, math.pi / NT) * delta
                    mag = jnp.sin(theta * span) / (NT * jnp.sin(theta))
                    gates.append(((mag * jnp.cos(phase))[0:1], (mag * jnp.sin(phase))[0:1] * plus))
            size = rows // ZPARTS
            pieces = []
            for part, direct, crossed in collect(vt, asent, agot, 1, step, -1, ZPARTS):
                z = model[part * size:(part + 1) * size] - stepping[...] * (direct - crossed)
                zsent[step, pl.ds(part * size, size)] = z.astype(BF16)
                for other in range(1, nfreq):
                    freq_copy(step, other, part).start()
                pieces.append(own_gate * z)
            for part in range(ZPARTS):
                for other in range(1, nfreq):
                    freq_copy(step, other, part).wait_recv()
                    zg = zgot[step, other - 1, pl.ds(part * size, size)].astype(F32)
                    gre, gim = gates[other - 1]
                    pieces[part] += gre * zg + gim * pltpu.roll(zg, half, 1)
            model = jnp.concatenate(pieces, axis=0)
        out[...] = model

        for step in range(ITERS):
            for other in range(1, nfreq):
                for part in range(ZPARTS):
                    freq_copy(step, other, part).wait_send()
            for place, off in enumerate(order):
                if off == 0:
                    continue

                @pl.when(inside(me + off))
                def _():
                    hop(fsent, fgot, 0, step, place, me).wait_send()

                @pl.when(inside(me - off))
                def _():
                    hop(asent, agot, 1, step, place, me).wait_send()

    return kernel


def on_device(model_start, data, col_factors, row_factors, ranks, gate_window, step_sizes):
    ntile = lax.axis_size("tile")
    nfreq = lax.axis_size("freq")
    slots, _, levels, rows = col_factors.shape[1:]
    width = model_start.shape[-1]
    any_space = pl.BlockSpec(memory_space=pl.ANY)
    block = (ITERS, slots * levels, width)
    peers = max(nfreq - 1, 1)
    result = pl.pallas_call(
        make_kernel(ntile, nfreq, slots, levels, rows, width),
        name="gradient_steps",
        out_shape=pltpu.VMEM((rows, width), F32),
        in_specs=[any_space] * 7,
        out_specs=pl.BlockSpec(memory_space=pltpu.VMEM),
        scratch_shapes=[
            pltpu.SMEM((slots, ntile), jnp.int32),
            pltpu.VMEM((2, width // 2), jnp.int32),
            pltpu.VMEM((1, 1), F32),
            pltpu.VMEM((rows, width), F32),
            pltpu.VMEM((rows, width), BF16),
            pltpu.VMEM((slots * levels, 2 * rows), BF16),
            pltpu.VMEM((slots * levels, 2 * rows), BF16),
            pltpu.VMEM((GROUPS, 2 * rows, slots * levels // GROUPS), BF16),
            pltpu.VMEM((GROUPS, 2 * rows, slots * levels // GROUPS), BF16),
            pltpu.VMEM(block, BF16),
            pltpu.VMEM(block, BF16),
            pltpu.VMEM(block, BF16),
            pltpu.VMEM(block, BF16),
            pltpu.VMEM((ITERS, rows, width), BF16),
            pltpu.VMEM((ITERS, peers, rows, width), BF16),
            pltpu.SemaphoreType.DMA((5,)),
            pltpu.SemaphoreType.DMA((slots, 2)),
            pltpu.SemaphoreType.DMA((slots, 2)),
            pltpu.SemaphoreType.DMA((ITERS, 2, slots)),
            pltpu.SemaphoreType.DMA((ITERS, 2, slots)),
            pltpu.SemaphoreType.DMA((ITERS, peers, ZPARTS)),
            pltpu.SemaphoreType.DMA((ITERS, peers, ZPARTS)),
        ],
        compiler_params=pltpu.CompilerParams(collective_id=0, has_side_effects=True),
    )(
        model_start[0], data[0], col_factors[0], row_factors[0], ranks[0].T, gate_window.T,
        step_sizes.reshape(1, 1),
    )
    return result[None]


def solution(mesh):
    return jax.shard_map(
        on_device,
        mesh=mesh,
        in_specs=(
            P("freq", "tile", None),
            P("freq", "tile", None),
            P("freq", "tile", None, None, None),
            P("freq", "tile", None, None, None),
            P("freq", None, None),
            P(),
            P("freq"),
        ),
        out_specs=P("freq", "tile", None),
        check_vma=False,
    )
```

time: 37.7 us -> 31.5 us (0.84)
  Pallas kernels: 33.1 us -> 30.1 us
  local copies, waits for them, and re-layouts: 3.63 us -> 0.66 us
    pallas_call x1, Pallas kernels: 33.1 us -> 30.1 us  [on_device(): pl.pallas_call(make_kernel(ntile, nfreq, slots, levels, rows, width), nam...]
    unnamed x6 -> x1, local copies, waits for them, and re-layouts: 2.97 us -> 0.66 us
    squeeze x1 -> x0, local copies, waits for them, and re-layouts: 0.67 us -> none  [on_device(): ranks[0]]
where the time goes in v2:
time: 31.5 us; the launch traced here: 31.4 us
  Pallas kernels  30.1 us (96%)
  local copies, waits for them, and re-layouts  0.66 us (2%)
  between operations  0.66 us (2%)
    pallas_call x1, Pallas kernels, on_device(): pl.pallas_call(make_kernel(ntile, nfreq, slots, levels, rows, width), nam...  30.1 us
    unnamed x1, local copies, waits for them, and re-layouts  0.66 us

profile of v2, /device:TPU:0, one launch (start us, length us, event | category | flops | bytes accessed | tf_op | source)
XLA Modules:
  0.0 31.4 jit_solution(8076502868262762250)
XLA Ops:
  0.7 30.1 %gradient_steps.1 = f32[256,128]{1,0:T(8,128)S(1)} custom-call(f32[256,128]{1,0:T(8,128)} %bitcast.14, bf16[256,128]{1,0:T(8,128)(2,1)} %bitcast.15, bf16[8,2,112,256]{3,2,1,0:T(8,128)(2,1)} %bitcast.12, bf16[8,2,112,256]{3,2,1,0:T(8,128)(2,1)} %bitcast.13, s32[8,16]{1,0:T(8,128)} %bitcast.16, s32[2,64]{1,0:T(2,128)} %bitcast.17, f32[1,1]{1,0:T(1,128)} %bitcast.10.stepping_hbm), custom_call_target="tpu_custom_call" | custom-call | tf_op jit(solution)/shard_map/gradient_steps/pallas_call | solution.py:270
  30.7 0.7 %copy.9 = f32[1,256,128]{2,1,0:T(8,128)} copy(f32[1,256,128]{2,1,0:T(8,128)S(1)} %bitcast.11) | data formatting | bytes 262144

commit v3 on v2

--- a/solution.py
+++ b/solution.py
@@ -13,7 +13,8 @@
 BF16 = jnp.bfloat16
 GROUPS = 4
 ZPARTS = 2
-RECEIVE = (0, 1, 2, 3)
+RECEIVE = (0, 1)
+MERGE = 2
 
 
 def slot_order(slots):
@@ -153,7 +154,7 @@
             size = rows // parts
             totals = [jnp.zeros((size, width), F32) for _ in range(2 * parts)]
             for g in RECEIVE:
-                for place in groups[g]:
+                for place in [p for m in range(MERGE) for p in groups[g * MERGE + m]]:
                     off = heading * order[place]
                     if off == 0:
                         continue
@@ -162,7 +163,7 @@
                     def _():
                         hop(sent, got, phase, step, place, me).wait_recv()
 
-                values = got[step, pl.ds(g * group_rows, group_rows)]
+                values = got[step, pl.ds(g * MERGE * group_rows, MERGE * group_rows)]
                 for part in range(parts):
                     for side in range(2):
                         start = side * rows + part * size
@@ -193,7 +194,7 @@
                     for place in places:
                         for part in range(2):
                             load_u[2 * place + part].wait()
-                    ut[g] = jnp.transpose(u[pl.ds(g * group_rows, group_rows)])
+                    ut[g // MERGE, :, (g % MERGE) * group_rows:(g % MERGE + 1) * group_rows] = jnp.transpose(u[pl.ds(g * group_rows, group_rows)])
                 load_data.wait()
             (_, direct, crossed), = collect(ut, fsent, fgot, 0, step, 1, 1)
             resid = (direct + crossed - data_ref[...].astype(F32)).astype(BF16)
@@ -201,7 +202,7 @@
             spread(u, rr, asent, agot, 1, step, -1, no_wait)
             if step == 0:
                 for g in range(GROUPS):
-                    vt[g] = jnp.transpose(v[pl.ds(g * group_rows, group_rows)])
+                    vt[g // MERGE, :, (g % MERGE) * group_rows:(g % MERGE + 1) * group_rows] = jnp.transpose(v[pl.ds(g * group_rows, group_rows)])
                 load_window.wait()
                 load_step.wait()
                 wf = window[...].astype(F32)
@@ -281,8 +282,8 @@
             pltpu.VMEM((rows, width), BF16),
             pltpu.VMEM((slots * levels, 2 * rows), BF16),
             pltpu.VMEM((slots * levels, 2 * rows), BF16),
-            pltpu.VMEM((GROUPS, 2 * rows, slots * levels // GROUPS), BF16),
-            pltpu.VMEM((GROUPS, 2 * rows, slots * levels // GROUPS), BF16),
+            pltpu.VMEM((GROUPS // MERGE, 2 * rows, slots * levels // GROUPS * MERGE), BF16),
+            pltpu.VMEM((GROUPS // MERGE, 2 * rows, slots * levels // GROUPS * MERGE), BF16),
             pltpu.VMEM(block, BF16),
             pltpu.VMEM(block, BF16),
             pltpu.VMEM(block, BF16),

time: 31.5 us -> 31.4 us (level)
  no operation moved by 1% of the time
where the time goes in v3:
time: 31.4 us; the launch traced here: 31.3 us
  Pallas kernels  29.9 us (95%)
  local copies, waits for them, and re-layouts  0.66 us (2%)
  between operations  0.66 us (2%)
    pallas_call x1, Pallas kernels, on_device(): pl.pallas_call(make_kernel(ntile, nfreq, slots, levels, rows, width), nam...  29.9 us
    unnamed x1, local copies, waits for them, and re-layouts  0.66 us

profile of v3, /device:TPU:0, one launch (start us, length us, event | category | flops | bytes accessed | tf_op | source)
XLA Modules:
  0.0 31.3 jit_solution(13405885340723818318)
XLA Ops:
  0.7 29.9 %gradient_steps.1 = f32[256,128]{1,0:T(8,128)S(1)} custom-call(f32[256,128]{1,0:T(8,128)} %bitcast.14, bf16[256,128]{1,0:T(8,128)(2,1)} %bitcast.15, bf16[8,2,112,256]{3,2,1,0:T(8,128)(2,1)} %bitcast.12, bf16[8,2,112,256]{3,2,1,0:T(8,128)(2,1)} %bitcast.13, s32[8,16]{1,0:T(8,128)} %bitcast.16, s32[2,64]{1,0:T(2,128)} %bitcast.17, f32[1,1]{1,0:T(1,128)} %bitcast.10.stepping_hbm), custom_call_target="tpu_custom_call" | custom-call | tf_op jit(solution)/shard_map/gradient_steps/pallas_call | solution.py:271
  30.6 0.7 %copy.9 = f32[1,256,128]{2,1,0:T(8,128)} copy(f32[1,256,128]{2,1,0:T(8,128)S(1)} %bitcast.11) | data formatting | bytes 262144
